TPU v7x, 256 devices: a whole 4x4x8 slice. The times are simulated.
256 devices in a mesh: row: 8 (over x, core), col: 32 (over y, z).
Axes of the slice: x: 4, y: 4, z: 8, core: 2. Of those that a mesh axis runs over, the one named last changes fastest.
Arguments:
- grid_points: int32 [2, 6, 4096], P(None, None, 'row'), may hold values from 0 to 127
- variable: int32 [6, 4096], P(None, 'row'), may hold values from 0 to 2
Outputs:
- panel_factor: float32 [6, 4096, 1536], P(None, ('row', 'col'))
- trailing: float32 [6, 4096, 16384], P(None, 'row', 'col')
All inputs are finite; a program needn't handle non-finite values.
Results may differ from a plain program's by a relative error of at most 0.0042.
Values may be sent and summed in bfloat16 or wider, within the bound.
A program may use at most 128 MiB of HBM per device.

v0:
```python
import jax
import jax.numpy as jnp
from jax import lax
from jax.sharding import PartitionSpec as P

PANELS = 3
GRID = 128
range_scale = 0.05
nugget = 0.5
rho_first = 0.35
rho_second = 0.2
rho_third = 0.3
highest = lax.Precision.HIGHEST


def rows_first(arrays, axis, dims):
    turned = [jnp.moveaxis(a, dim, 0) for a, dim in zip(arrays, dims)]
    widths = [t[0].size for t in turned]
    both = jnp.concatenate([t.reshape(-1, w) for t, w in zip(turned, widths)], axis=1)
    whole = lax.all_gather(both, axis, axis=0, tiled=True)
    parts = jnp.split(whole, [sum(widths[:k]) for k in range(1, len(widths))], axis=1)
    return tuple(
        (
            jnp.moveaxis(b.reshape(-1, *t.shape[1:]), 0, dim)
            for b, t, dim in zip(parts, turned, dims)
        )
    )


def kind_scale(kinds):
    return jnp.where(kinds == 0, 1.0, jnp.where(kinds == 1, 1.3, 0.8))


def covariance(row_x, row_y, row_kind, col_x, col_y, col_kind):
    delta_x = (row_x[:, None] - col_x[None, :]).astype(jnp.float32)
    delta_y = (row_y[:, None] - col_y[None, :]).astype(jnp.float32)
    distance = jnp.sqrt(delta_x * delta_x + delta_y * delta_y) * (1.0 / (GRID * range_scale))
    order_sum = row_kind[:, None] + col_kind[None, :]
    dist_square = distance * distance
    dist_cube = dist_square * distance
    dist_fourth = dist_square * dist_square
    polynomial = jnp.where(order_sum == 0, 1.0, 1.0 + distance)
    polynomial = jnp.where(order_sum == 2, 1.0 + distance + dist_square / 3.0, polynomial)
    polynomial = jnp.where(
        order_sum == 3, 1.0 + distance + 0.4 * dist_square + dist_cube / 15.0, polynomial
    )
    polynomial = jnp.where(
        order_sum == 4,
        1.0 + distance + dist_square * (3.0 / 7.0) + dist_cube * (2.0 / 21.0) + dist_fourth / 105.0,
        polynomial,
    )
    correlation = jnp.where(
        row_kind[:, None] == col_kind[None, :],
        1.0,
        jnp.where(order_sum == 1, rho_first, jnp.where(order_sum == 2, rho_second, rho_third)),
    )
    scale_row = kind_scale(row_kind)
    scale_col = kind_scale(col_kind)
    return correlation * scale_row[:, None] * scale_col[None, :] * polynomial * jnp.exp(-distance)


def leading_factor(matrix, count, size):
    remaining = matrix
    lower_blocks = {}
    inverse_blocks = {}
    identity = jnp.eye(size, dtype=jnp.float32)
    for panel_step in range(count):
        row_begin = panel_step * size
        row_end = row_begin + size
        diag_factor = jnp.linalg.cholesky(remaining[row_begin:row_end, row_begin:row_end])
        diag_inverse = lax.linalg.triangular_solve(
            diag_factor, identity, left_side=True, lower=True
        )
        lower_blocks[panel_step, panel_step] = diag_factor
        inverse_blocks[panel_step, panel_step] = diag_inverse
        if panel_step + 1 < count:
            below_rows = jnp.dot(
                remaining[row_end:, row_begin:row_end], diag_inverse.T, precision=highest
            )
            for row_block in range(panel_step + 1, count):
                lower_blocks[row_block, panel_step] = below_rows[
                    (row_block - panel_step - 1) * size : (row_block - panel_step) * size
                ]
            trailing_part = remaining[row_end:, row_end:] - jnp.dot(
                below_rows, below_rows.T, precision=highest
            )
            remaining = remaining.at[row_end:, row_end:].set(trailing_part)
    for row_block in range(count):
        for col_block in range(row_block):
            running = jnp.zeros((size, size), jnp.float32)
            for mid_block in range(col_block, row_block):
                running = running + jnp.dot(
                    lower_blocks[row_block, mid_block],
                    inverse_blocks[mid_block, col_block],
                    precision=highest,
                )
            inverse_blocks[row_block, col_block] = -jnp.dot(
                inverse_blocks[row_block, row_block], running, precision=highest
            )
    zeros_block = jnp.zeros((size, size), jnp.float32)
    lower_rows = []
    inverse_rows = []
    for row_block in range(count):
        lower_rows.append(
            jnp.concatenate(
                [
                    lower_blocks[row_block, col_block] if col_block <= row_block else zeros_block
                    for col_block in range(count)
                ],
                1,
            )
        )
        inverse_rows.append(
            jnp.concatenate(
                [
                    inverse_blocks[row_block, col_block] if col_block <= row_block else zeros_block
                    for col_block in range(count)
                ],
                1,
            )
        )
    return (jnp.concatenate(lower_rows, 0), jnp.concatenate(inverse_rows, 0))


def local(grid_points, variable):
    rows_dev = variable.shape[0]
    tile_size = variable.shape[1]
    row_count = lax.axis_size("row")
    col_count = lax.axis_size("col")
    piece_rows = tile_size // col_count
    row_index = lax.axis_index("row")
    col_index = lax.axis_index("col")
    lead_size = PANELS * tile_size
    all_grid, all_kind = rows_first((grid_points, variable), "row", (2, 1))
    coord_x = all_grid[0].reshape(-1)
    coord_y = all_grid[1].reshape(-1)
    kinds = all_kind.reshape(-1)
    lead_x = coord_x[:lead_size]
    lead_y = coord_y[:lead_size]
    lead_kind = kinds[:lead_size]
    lead_cov = covariance(lead_x, lead_y, lead_kind, lead_x, lead_y, lead_kind)
    lead_cov = lead_cov + nugget * jnp.eye(lead_size, dtype=jnp.float32)
    lower_factor, inverse = leading_factor(lead_cov, PANELS, tile_size)
    offset = col_index * piece_rows
    mine_grid = lax.dynamic_slice_in_dim(grid_points, offset, piece_rows, 2)
    mine_kind = lax.dynamic_slice_in_dim(variable, offset, piece_rows, 1)
    piece_cov = covariance(
        mine_grid[0].reshape(-1),
        mine_grid[1].reshape(-1),
        mine_kind.reshape(-1),
        lead_x,
        lead_y,
        lead_kind,
    )
    solved = jnp.dot(piece_cov, inverse.T, precision=highest).reshape(
        rows_dev, piece_rows, lead_size
    )
    lead_rows = lax.dynamic_slice_in_dim(
        lower_factor,
        jnp.minimum(row_index * tile_size + offset, lead_size - piece_rows),
        piece_rows,
        0,
    )
    first_slot = jnp.where(row_index < PANELS, lead_rows, solved[0])
    panel_full = jnp.concatenate([first_slot[None], solved[1:]], 0)
    panel_half = panel_full.astype(jnp.bfloat16)
    target = PANELS + col_index
    col_start = target * tile_size
    col_x = lax.dynamic_slice_in_dim(coord_x, col_start, tile_size)
    col_y = lax.dynamic_slice_in_dim(coord_y, col_start, tile_size)
    col_kind = lax.dynamic_slice_in_dim(kinds, col_start, tile_size)
    row_iota = lax.broadcasted_iota(jnp.int32, (tile_size, tile_size), 0)
    col_iota = lax.broadcasted_iota(jnp.int32, (tile_size, tile_size), 1)

    def assemble(slot):
        cov_block = covariance(
            grid_points[0][slot], grid_points[1][slot], variable[slot], col_x, col_y, col_kind
        )
        equal = (slot * row_count + row_index == target) & (row_iota == col_iota)
        return jnp.where(equal, cov_block + nugget, cov_block)

    cov_tiles = lax.map(assemble, jnp.arange(rows_dev, dtype=jnp.int32))
    target_cov = covariance(col_x, col_y, col_kind, lead_x, lead_y, lead_kind)
    column_rows = jnp.dot(target_cov, inverse.T, precision=highest).astype(jnp.bfloat16)
    update = jnp.einsum(
        "sik,jk->sij",
        lax.all_gather(panel_half, "col", axis=1, tiled=True),
        column_rows,
        preferred_element_type=jnp.float32,
    )
    return (panel_full, cov_tiles - update)


def solution(mesh):
    return jax.shard_map(
        local,
        mesh=mesh,
        in_specs=(P(None, None, "row"), P(None, "row")),
        out_specs=(P(None, ("row", "col"), None), P(None, "row", "col")),
        check_vma=False,
    )
```

profile of v0, /device:TPU:1, one launch (start us, length us, event | category | flops | bytes accessed | tf_op | source)
XLA Modules:
  0.0 741.4 jit_solution(12981079836239768969)
XLA Ops:
  8.7 16.0 %all_gather.6 = s32[4096,18]{0,1:T(8,128)S(1)} all-gather(s32[512,18]{0,1:T(8,128)S(1)} %pad_add_fusion), channel_id=1, replica_groups=mesh['row'=8,'col'=32] {'row'}, dimensions={0}, use_global_device_ids=true | all-gather | bytes 331776 | tf_op jit(solution)/shard_map/all_gather | solution.py:20
  25.8 18.3 %fusion.28 = f32[1536,1536]{0,1:T(8,128)S(1)} fusion(s32[1536]{0:T(1024)S(1)} %slice.297, s32[1536]{0:T(1024)S(1)} %slice.295, f32[1536]{0:T(1024)S(1)} %select_select_fusion.5, s32[1536]{0:T(1024)S(1)} %slice.293), kind=kLoop, calls=%fused_computation.64 | loop fusion | flops 108527616 | bytes 9461760 | tf_op jit(solution)/shard_map/add | solution.py:142
  44.2 3.6 copy-done
  49.7 11.7 %cholesky.374 = f32[128,128]{1,0:T(8,128)S(1)} custom-call(f32[128,128]{1,0:T(8,128)S(1)} %cholesky.586), custom_call_target="Cholesky" | custom-call | tf_op jit(solution)/shard_map/jit(cholesky)/cholesky | solution.py:70
  61.5 9.8 %custom-call.31 = f32[1,128,128]{1,2,0:T(8,128)S(1)} custom-call(f32[1,128,128]{2,1,0:T(8,128)S(1)} %get-tuple-element.310), custom_call_target="InvertDiagBlocksLowerTriangular" | custom-call | tf_op jit(solution)/shard_map/jit(cholesky)/cholesky | solution.py:70
  72.1 11.7 %cholesky.393 = f32[128,128]{1,0:T(8,128)S(1)} custom-call(f32[128,128]{1,0:T(8,128)S(1)} %cholesky.590), custom_call_target="Cholesky" | custom-call | tf_op jit(solution)/shard_map/jit(cholesky)/cholesky | solution.py:70
  83.8 10.2 %custom-call.32 = f32[1,128,128]{1,2,0:T(8,128)S(1)} custom-call(f32[1,128,128]{2,1,0:T(8,128)S(1)} %get-tuple-element.307), custom_call_target="InvertDiagBlocksLowerTriangular" | custom-call | tf_op jit(solution)/shard_map/jit(cholesky)/cholesky | solution.py:70
  94.7 11.7 %cholesky.414 = f32[128,128]{1,0:T(8,128)S(1)} custom-call(f32[128,128]{1,0:T(8,128)S(1)} %cholesky.595), custom_call_target="Cholesky" | custom-call | tf_op jit(solution)/shard_map/jit(cholesky)/cholesky | solution.py:70
  107.1 9.8 %custom-call.33 = f32[1,128,128]{1,2,0:T(8,128)S(1)} custom-call(f32[1,128,128]{2,1,0:T(8,128)S(1)} %get-tuple-element.304), custom_call_target="InvertDiagBlocksLowerTriangular" | custom-call | tf_op jit(solution)/shard_map/jit(cholesky)/cholesky | solution.py:70
  117.5 11.7 %cholesky.431 = f32[128,128]{1,0:T(8,128)S(1)} custom-call(f32[128,128]{1,0:T(8,128)S(1)} %convolution_subtract_fusion.19), custom_call_target="Cholesky" | custom-call | tf_op jit(solution)/shard_map/jit(cholesky)/cholesky | solution.py:70
  134.6 7.9 %while.22 = (s32[]{:T(128)}, f32[512,512]{1,0:T(8,128)S(1)}, s32[4,2]{0,1:T(2,128)S(1)}, f32[4,128,128]{2,1,0:T(8,128)S(1)}, s32[]{:T(128)}) while((s32[]{:T(128)}, f32[512,512]{1,0:T(8,128)S(1)}, s32[4,2]{0,1:T(2,128)S(1)}, f32[4,128,128]{2,1,0:T(8,128)S(1)}, s32[]{:T(128)}) %tuple.122), condition=%wide.while_cond.2, body=%wide.while_body.2.sunk | while | flops 2 | bytes 131181 | solution.py:71
  142.5 39.3 %custom-call.34 = f32[4,128,128]{1,2,0:T(8,128)S(1)} custom-call(f32[4,128,128]{2,1,0:T(8,128)S(1)} %get-tuple-element.206), custom_call_target="InvertDiagBlocksLowerTriangular" | custom-call | tf_op jit(solution)/shard_map/triangular_solve/custom-call.3 | solution.py:71
  185.0 5.2 fusion.82
  190.3 2.8 fusion.314
  193.1 9.2 %slice_subtract_fusion = f32[1024,1024]{0,1:T(8,128)S(1)} fusion(f32[1536,1536]{0,1:T(8,128)} %copy-done, f32[1024,512]{0,1:T(8,128)S(1)} %fusion.82), kind=kOutput, calls=%fused_computation.90 | convolution fusion | flops 6443499520 | bytes 12582912 | tf_op jit(solution)/shard_map/dot_general | solution.py:84
  205.4 2.6 copy.26
  210.8 11.7 %cholesky.446 = f32[128,128]{1,0:T(8,128)S(1)} custom-call(f32[128,128]{1,0:T(8,128)S(1)} %cholesky.599), custom_call_target="Cholesky" | custom-call | tf_op jit(solution)/shard_map/jit(cholesky)/cholesky | solution.py:70
  223.2 10.6 %custom-call.35 = f32[1,128,128]{1,2,0:T(8,128)S(1)} custom-call(f32[1,128,128]{2,1,0:T(8,128)} %get-tuple-element.300), custom_call_target="InvertDiagBlocksLowerTriangular" | custom-call | tf_op jit(solution)/shard_map/jit(cholesky)/cholesky | solution.py:70
  237.6 2.2 convolution_subtract_fusion.12
  239.8 3.9 fusion.312
  245.7 11.9 %cholesky.465 = f32[128,128]{1,0:T(8,128)S(1)} custom-call(f32[128,128]{1,0:T(8,128)S(1)} %cholesky.603), custom_call_target="Cholesky" | custom-call | tf_op jit(solution)/shard_map/jit(cholesky)/cholesky | solution.py:70
  261.1 9.8 %custom-call.36 = f32[1,128,128]{1,2,0:T(8,128)S(1)} custom-call(f32[1,128,128]{2,1,0:T(8,128)S(1)} %get-tuple-element.297), custom_call_target="InvertDiagBlocksLowerTriangular" | custom-call | tf_op jit(solution)/shard_map/jit(cholesky)/cholesky | solution.py:70
  274.2 11.7 %cholesky.486 = f32[128,128]{1,0:T(8,128)S(1)} custom-call(f32[128,128]{1,0:T(8,128)S(1)} %cholesky.608), custom_call_target="Cholesky" | custom-call | tf_op jit(solution)/shard_map/jit(cholesky)/cholesky | solution.py:70
  287.3 9.8 %custom-call.37 = f32[1,128,128]{1,2,0:T(8,128)S(1)} custom-call(f32[1,128,128]{2,1,0:T(8,128)S(1)} %get-tuple-element.294), custom_call_target="InvertDiagBlocksLowerTriangular" | custom-call | tf_op jit(solution)/shard_map/jit(cholesky)/cholesky | solution.py:70
  299.4 12.1 %cholesky.503 = f32[128,128]{1,0:T(8,128)S(1)} custom-call(f32[128,128]{1,0:T(8,128)S(1)} %convolution_subtract_fusion.18), custom_call_target="Cholesky" | custom-call | tf_op jit(solution)/shard_map/jit(cholesky)/cholesky | solution.py:70
  315.3 2.9 fusion.114
  318.3 10.8 %while.23 = (s32[]{:T(128)}, f32[512,512]{1,0:T(8,128)}, s32[4,2]{0,1:T(2,128)S(1)}, f32[4,128,128]{2,1,0:T(8,128)S(1)}, s32[]{:T(128)}) while((s32[]{:T(128)}, f32[512,512]{1,0:T(8,128)}, s32[4,2]{0,1:T(2,128)S(1)}, f32[4,128,128]{2,1,0:T(8,128)S(1)}, s32[]{:T(128)}) %tuple.137), condition=%wide.while_cond.2.clone, body=%wide.while_body.2.clone.sunk | while | flops 2 | bytes 131181 | solution.py:71
  329.1 39.9 %custom-call.38 = f32[4,128,128]{1,2,0:T(8,128)} custom-call(f32[4,128,128]{2,1,0:T(8,128)S(1)} %get-tuple-element.207), custom_call_target="InvertDiagBlocksLowerTriangular" | custom-call | tf_op jit(solution)/shard_map/triangular_solve/custom-call.3 | solution.py:71
  378.5 3.2 fusion.108
  381.7 4.2 convolution_subtract_fusion.1
  385.9 2.5 copy.32
  391.2 11.7 %cholesky.518 = f32[128,128]{1,0:T(8,128)S(1)} custom-call(f32[128,128]{1,0:T(8,128)S(1)} %cholesky.612), custom_call_target="Cholesky" | custom-call | tf_op jit(solution)/shard_map/jit(cholesky)/cholesky | solution.py:70
  403.6 10.8 %custom-call.39 = f32[1,128,128]{1,2,0:T(8,128)S(1)} custom-call(f32[1,128,128]{2,1,0:T(8,128)} %get-tuple-element.290), custom_call_target="InvertDiagBlocksLowerTriangular" | custom-call | tf_op jit(solution)/shard_map/jit(cholesky)/cholesky | solution.py:70
  418.1 2.2 convolution_subtract_fusion.11
  420.3 4.0 fusion.223
  429.4 4.4 convolution_negate_fusion.2
  433.9 11.7 %cholesky.537 = f32[128,128]{1,0:T(8,128)S(1)} custom-call(f32[128,128]{1,0:T(8,128)S(1)} %slice-done), custom_call_target="Cholesky" | custom-call | tf_op jit(solution)/shard_map/jit(cholesky)/cholesky | solution.py:70
  447.9 10.0 %custom-call.40 = f32[1,128,128]{1,2,0:T(8,128)S(1)} custom-call(f32[1,128,128]{2,1,0:T(8,128)S(1)} %get-tuple-element.287), custom_call_target="InvertDiagBlocksLowerTriangular" | custom-call | tf_op jit(solution)/shard_map/jit(cholesky)/cholesky | solution.py:70
  461.0 13.2 %cholesky.558 = f32[128,128]{1,0:T(8,128)} custom-call(f32[128,128]{1,0:T(8,128)} %cholesky.621), custom_call_target="Cholesky" | custom-call | tf_op jit(solution)/shard_map/jit(cholesky)/cholesky | solution.py:70
  476.3 11.3 %custom-call.41 = f32[1,128,128]{1,2,0:T(8,128)} custom-call(f32[1,128,128]{2,1,0:T(8,128)} %get-tuple-element.284), custom_call_target="InvertDiagBlocksLowerTriangular" | custom-call | tf_op jit(solution)/shard_map/jit(cholesky)/cholesky | solution.py:70
  489.9 11.7 %cholesky.575 = f32[128,128]{1,0:T(8,128)S(1)} custom-call(f32[128,128]{1,0:T(8,128)S(1)} %convolution_subtract_fusion.17), custom_call_target="Cholesky" | custom-call | tf_op jit(solution)/shard_map/jit(cholesky)/cholesky | solution.py:70
  506.3 12.0 %while.24 = (s32[]{:T(128)}, f32[512,512]{1,0:T(8,128)}, s32[4,2]{0,1:T(2,128)S(1)}, f32[4,128,128]{2,1,0:T(8,128)S(1)}, s32[]{:T(128)}) while((s32[]{:T(128)}, f32[512,512]{1,0:T(8,128)}, s32[4,2]{0,1:T(2,128)S(1)}, f32[4,128,128]{2,1,0:T(8,128)S(1)}, s32[]{:T(128)}) %tuple.138), condition=%wide.while_cond.2.clone.1, body=%wide.while_body.2.clone.1.sunk | while | flops 2 | bytes 131181 | solution.py:71
  507.0 2.3 bitcast_dynamic-update-slice_fusion.8
  510.0 2.3 bitcast_dynamic-update-slice_fusion.8
  513.0 2.3 bitcast_dynamic-update-slice_fusion.8
  516.1 2.3 bitcast_dynamic-update-slice_fusion.8
  518.3 39.7 %custom-call.42 = f32[4,128,128]{1,2,0:T(8,128)S(1)} custom-call(f32[4,128,128]{2,1,0:T(8,128)S(1)} %get-tuple-element.208), custom_call_target="InvertDiagBlocksLowerTriangular" | custom-call | tf_op jit(solution)/shard_map/triangular_solve/custom-call.3 | solution.py:71
  565.8 3.4 convolution_add_fusion
  569.2 2.8 convolution_negate_fusion.1
  572.0 2.9 convolution_negate_fusion
  576.1 2.5 copy.49
  578.6 2.6 copy.50
  581.3 20.2 %fusion.38 = f32[1536,1536]{1,0:T(8,128)} fusion(f32[512,512]{1,0:T(8,128)S(1)} %cholesky.441, f32[512,512]{1,0:T(8,128)} %pad_maximum_fusion.1, f32[128,512]{1,0:T(8,128)S(1)} %fusion.240, f32[128,512]{1,0:T(8,128)} %copy-done.12, f32[128,512]{1,0:T(8,128)S(1)} %fusion.243, f32[128,512]{1,0:T(8,128)S(1)} %fusion.205, f32[512,512]{1,0:T(8,128)} %convolution_negate_fusion, ...), kind=kLoop, calls=%fused_computation.76 | loop fusion | flops 33030144 | bytes 16777216 | tf_op jit(solution)/shard_map/concatenate | solution.py:122
  601.6 13.2 %fusion.140 = f32[96,1536]{1,0:T(8,128)S(1)} fusion(f32[1536,1536]{1,0:T(8,128)} %fusion.38, s32[1536]{0:T(1024)S(1)} %copy-done.28, s32[96]{0:T(128)S(1)} %sub.151, s32[1536]{0:T(1024)S(1)} %copy-done.26, s32[96]{0:T(128)S(1)} %sub.147, f32[1536]{0:T(1024)S(1)} %select_select_fusion.5, f32[96]{0:T(128)S(1)} %compare_select_fusion.1, ...), kind=kOutput, calls=%fused_computation.241 | convolution fusion | flops 2724249600 | bytes 10053120 | tf_op jit(solution)/shard_map/dot_general | solution.py:155
  621.8 28.3 %fusion.79 = bf16[512,1536,1]{1,0,2:T(8,128)(2,1)S(1)} fusion(f32[1536,1536]{1,0:T(8,128)} %fusion.38, s32[1536]{0:T(1024)S(1)} %copy-done.28, s32[512]{0:T(512)S(1)} %dynamic_slice.42, s32[1536]{0:T(1024)S(1)} %copy-done.26, s32[512]{0:T(512)S(1)} %dynamic_slice.41, f32[1536]{0:T(1024)S(1)} %select_select_fusion.5, f32[512]{0:T(512)S(1)} %get-tuple-element.255, ...), kind=kOutput, calls=%fused_computation.131 | convolution fusion | flops 14530117632 | bytes 11042816 | tf_op jit(solution)/shard_map/dot_general | solution.py:184
  650.1 42.0 %while.21 = (s32[]{:T(128)}, f32[6,512,512]{2,1,0:T(8,128)}, s32[6]{0:T(128)S(1)}, s32[]{:T(128)}, s32[]{:T(128)}, /*index=5*/s32[6,512]{1,0:T(8,128)}, s32[512]...) while((s32[]{:T(128)}, f32[6,512,512]{2,1,0:T(8,128)}, ...), condition=%wide.region_9.12_spmd.clone, body=%wide.region_8.11_spmd.clone.sunk | while | flops 12324872 | bytes 1135325 | solution.py:182
  654.3 3.0 fusion.358
  661.2 3.0 fusion.358
  668.2 3.0 fusion.358
  675.1 3.0 fusion.358
  682.1 3.0 fusion.358
  689.0 3.0 fusion.358
  692.0 30.6 %all-gather.2.cloned.1.call-done = bf16[6,512,1536]{2,1,0:T(8,128)(2,1)} async-done(((bf16[6,16,1536]{2,1,0:T(8,128)(2,1)}), bf16[6,512,1536]{2,1,0:T(8,128)(2,1)}) %all-gather.2.cloned.1.call-update) | async-done | bytes 9437200 | tf_op jit(solution)/shard_map/all_gather | solution.py:187
  722.6 11.6 %convolution_subtract_fusion = f32[6,512,512]{2,1,0:T(8,128)} fusion(f32[6,512,512]{2,1,0:T(8,128)} %get-tuple-element.163, bf16[6,512,1536]{2,1,0:T(8,128)(2,1)} %all-gather.2.cloned.1.call-done, bf16[512,1536,1]{1,0,2:T(8,128)(2,1)S(1)} %fusion.79), kind=kOutput, calls=%fused_computation.132 | convolution fusion | flops 4833411072 | bytes 23592960 | tf_op jit(solution)/shard_map/sik,jk->sij/dot_general | solution.py:185
  (248 shorter events, 116.3 us)
Async XLA Ops:
  7.2 715.5 %all-gather.2.cloned.1.call-start = ((), (), s32[]{:S(2)}) async-start(), calls=%async_computation | async-start | bytes 9732096 | tf_op jit(solution)/shard_map/all_gather | solution.py:187
  24.8 0.6 copy-start.22
  25.4 18.7 %copy-start.23 = (s32[1536]{0:T(1024)}, s32[1536]{0:T(1024)S(1)}, u32[]{:S(2)}) copy-start(s32[1536]{0:T(1024)S(1)} %slice.293) | copy-start | bytes 18436
  25.6 349.9 %copy-start.2 = (f32[512,512]{1,0:T(8,128)}, f32[512,512]{1,0:T(8,128)S(1)}, u32[]{:S(2)}) copy-start(f32[512,512]{1,0:T(8,128)S(1)} %fusion.116) | copy-start | bytes 3145732
  25.7 18.5 %copy-start.29 = (s32[24576]{0:T(1024)}, s32[24576]{0:T(1024)S(1)}, u32[]{:S(2)}) copy-start(s32[24576]{0:T(1024)S(1)} %reshape_squeeze.6) | copy-start | bytes 294916
  25.7 18.5 %copy-start.25 = (s32[1536]{0:T(1024)}, s32[1536]{0:T(1024)S(1)}, u32[]{:S(2)}) copy-start(s32[1536]{0:T(1024)S(1)} %slice.295) | copy-start | bytes 18436
  25.8 18.4 %copy-start.30 = (s32[24576]{0:T(1024)}, s32[24576]{0:T(1024)S(1)}, u32[]{:S(2)}) copy-start(s32[24576]{0:T(1024)S(1)} %reshape_squeeze.7) | copy-start | bytes 294916
  25.8 18.4 %copy-start.27 = (s32[1536]{0:T(1024)}, s32[1536]{0:T(1024)S(1)}, u32[]{:S(2)}) copy-start(s32[1536]{0:T(1024)S(1)} %slice.297) | copy-start | bytes 18436
  44.2 3.6 copy-start
  182.3 57.6 %copy-start.4 = (f32[128,512]{1,0:T(8,128)}, f32[128,512]{1,0:T(8,128)S(1)}, u32[]{:S(2)}) copy-start(f32[128,512]{1,0:T(8,128)S(1)} %fusion.209) | copy-start | bytes 786436
  183.1 7.2 copy-start.7
  183.9 6.3 copy-start.10
  185.0 5.3 copy-start.13
  202.3 2.0 copy-start.1
  209.8 1.1 copy-start.18
  372.8 5.7 copy-start.5
  375.5 6.2 copy-start.8
  378.5 3.2 copy-start.11
  390.2 1.0 copy-start.17
  420.3 13.6 %slice-start = ((f32[384,128]{1,0:T(8,128)}), f32[128,128]{1,0:T(8,128)S(1)}, s32[]{:S(2)}) async-start(f32[384,128]{1,0:T(8,128)} %convolution_subtract_fusion.11), calls=%async_computation.1 | async-start | bytes 131072 | tf_op jit(solution)/shard_map/jit(cholesky)/cholesky | solution.py:70
  429.4 128.6 %copy-start.3 = (f32[512,512]{1,0:T(8,128)S(1)}, f32[512,512]{1,0:T(8,128)}, u32[]{:S(2)}) copy-start(f32[512,512]{1,0:T(8,128)} %copy-done.2) | copy-start | bytes 3145732
  506.3 69.4 %copy-start.20 = (s32[2,6,512]{2,0,1:T(2,128)S(1)}, s32[2,6,512]{2,0,1:T(2,128)}, u32[]{:S(2)}) copy-start(s32[2,6,512]{2,0,1:T(2,128)} %param.11) | copy-start | bytes 73732
  558.1 2.1 copy-start.21
  558.1 14.0 %copy-start.14 = (f32[512,512]{1,0:T(8,128)S(1)}, f32[512,512]{1,0:T(8,128)}, u32[]{:S(2)}) copy-start(f32[512,512]{1,0:T(8,128)} %fusion.223) | copy-start | bytes 3145732
  561.5 19.8 %copy-start.6 = (f32[128,512]{1,0:T(8,128)S(1)}, f32[128,512]{1,0:T(8,128)}, u32[]{:S(2)}) copy-start(f32[128,512]{1,0:T(8,128)} %copy-done.5) | copy-start | bytes 786436
  561.5 19.8 %copy-start.9 = (f32[128,512]{1,0:T(8,128)S(1)}, f32[128,512]{1,0:T(8,128)}, u32[]{:S(2)}) copy-start(f32[128,512]{1,0:T(8,128)} %copy-done.8) | copy-start | bytes 786436
  562.9 9.2 %copy-start.12 = (f32[128,512]{1,0:T(8,128)}, f32[128,512]{1,0:T(8,128)S(1)}, u32[]{:S(2)}) copy-start(f32[128,512]{1,0:T(8,128)S(1)} %fusion.241) | copy-start | bytes 786436
  581.2 20.4 %copy-start.24 = (s32[1536]{0:T(1024)S(1)}, s32[1536]{0:T(1024)}, u32[]{:S(2)}) copy-start(s32[1536]{0:T(1024)} %copy-done.23) | copy-start | bytes 18436
  581.2 20.4 %copy-start.26 = (s32[1536]{0:T(1024)S(1)}, s32[1536]{0:T(1024)}, u32[]{:S(2)}) copy-start(s32[1536]{0:T(1024)} %copy-done.25) | copy-start | bytes 18436
  581.2 20.4 %copy-start.28 = (s32[1536]{0:T(1024)S(1)}, s32[1536]{0:T(1024)}, u32[]{:S(2)}) copy-start(s32[1536]{0:T(1024)} %copy-done.27) | copy-start | bytes 18436
  601.5 14.9 %copy-start.15 = (f32[512,512]{1,0:T(8,128)S(1)}, f32[512,512]{1,0:T(8,128)}, u32[]{:S(2)}) copy-start(f32[512,512]{1,0:T(8,128)} %get-tuple-element.264) | copy-start | bytes 3145732
  601.6 14.9 %copy-start.16 = (f32[512,512]{1,0:T(8,128)S(1)}, f32[512,512]{1,0:T(8,128)}, u32[]{:S(2)}) copy-start(f32[512,512]{1,0:T(8,128)} %get-tuple-element.262) | copy-start | bytes 3145732
  614.8 0.8 copy-start.19
Sparse Core Ops, SparseCore 0:
  619.6 102.9 all-gather.1
where the time goes:
time: 750 us; the launch traced here: 741 us
  other arithmetic  440 us (59%)
  matrix products  140 us (19%)
  local copies, waits for them, and re-layouts  76.1 us (10%)
  waiting for transfers between devices  30.6 us (4%)
  between operations  22.7 us (3%)
  blocking collectives  16 us (2%)
  loops' own time  15.8 us (2%)
    another operation x44, other arithmetic, leading_factor(): jnp.linalg.cholesky(remaining[row_begin:row_end, row_begin:row_end])  247 us
    another operation x8, other arithmetic, leading_factor(): lax.linalg.triangular_solve(diag_factor, identity, left_side=True, lower=...  127 us
    another operation x40, local copies, waits for them, and re-layouts, leading_factor(): lax.linalg.triangular_solve(diag_factor, identity, left_side=True, lower=...  30.6 us
    all_gather x1, waiting for transfers between devices, local(): lax.all_gather(panel_half, 'col', axis=1, tiled=True)  30.6 us
    dot_general x1, matrix products, local(): jnp.dot(target_cov, inverse.T, precision=highest).astype(jnp.bfloat16)  28.3 us
    another operation x18, matrix products, leading_factor(): jnp.linalg.cholesky(remaining[row_begin:row_end, row_begin:row_end])  20.6 us
    concatenate x1, other arithmetic, leading_factor(): return (jnp.concatenate(lower_rows, 0), jnp.concatenate(inverse_rows, 0))  20.2 us
    another operation x21, matrix products, leading_factor(): lax.linalg.triangular_solve(diag_factor, identity, left_side=True, lower=...  20 us
  transfers between devices with their start and end apart: 1, of which 1 were waited for; matrix products, arithmetic and copies ran while one was open for 8% of the time, Pallas kernels for 0%

commit v1 on v0

--- a/solution.py
+++ b/solution.py
@@ -184,7 +184,9 @@
     column_rows = jnp.dot(target_cov, inverse.T, precision=highest).astype(jnp.bfloat16)
     update = jnp.einsum(
         "sik,jk->sij",
-        lax.all_gather(panel_half, "col", axis=1, tiled=True),
+        jnp.concatenate(
+            lax.all_to_all(jnp.stack([panel_half] * lax.axis_size("col")), "col", 0, 0), axis=1
+        ),
         column_rows,
         preferred_element_type=jnp.float32,
     )

time: 750 us -> 877 us (1.17)
  waiting for transfers between devices: 30.6 us -> 142 us
  local copies, waits for them, and re-layouts: 76.1 us -> 90.9 us
  between operations: 22.7 us -> 9.48 us
  starting transfers between devices: 0.04 us -> 10.2 us
    all_to_all x0 -> x1, waiting for transfers between devices: none -> 142 us  [local(): lax.all_to_all(jnp.stack([panel_half] * lax.axis_size('col')), 'col', 0, 0)]
    all_gather x1 -> x0, waiting for transfers between devices: 30.6 us -> none  [local(): lax.all_gather(panel_half, 'col', axis=1, tiled=True)]
    all_to_all x0 -> x1, starting transfers between devices: none -> 10.2 us  [local(): lax.all_to_all(jnp.stack([panel_half] * lax.axis_size('col')), 'col', 0, 0)]
  transfers between devices with their start and end apart: 1 -> 1, of which waited for: 1 -> 1; matrix products, arithmetic and copies ran while one was open for 8% -> 7% of each run, Pallas kernels for 0% -> 0%
where the time goes in v1:
time: 877 us; the launch traced here: 863 us
  other arithmetic  440 us (50%)
  waiting for transfers between devices  142 us (16%)
  matrix products  140 us (16%)
  local copies, waits for them, and re-layouts  90.9 us (10%)
  blocking collectives  16 us (2%)
  loops' own time  14.2 us (2%)
  starting transfers between devices  10.2 us (1%)
  between operations  9.48 us (1%)
    another operation x44, other arithmetic, leading_factor(): jnp.linalg.cholesky(remaining[row_begin:row_end, row_begin:row_end])  247 us
    all_to_all x1, waiting for transfers between devices, local(): lax.all_to_all(jnp.stack([panel_half] * lax.axis_size('col')), 'col', 0, 0)  142 us
    another operation x8, other arithmetic, leading_factor(): lax.linalg.triangular_solve(diag_factor, identity, left_side=True, lower=...  128 us
    another operation x40, local copies, waits for them, and re-layouts, leading_factor(): lax.linalg.triangular_solve(diag_factor, identity, left_side=True, lower=...  31.6 us
    dot_general x1, matrix products, local(): jnp.dot(target_cov, inverse.T, precision=highest).astype(jnp.bfloat16)  28.1 us
    another operation x18, matrix products, leading_factor(): jnp.linalg.cholesky(remaining[row_begin:row_end, row_begin:row_end])  21.5 us
    another operation x21, matrix products, leading_factor(): lax.linalg.triangular_solve(diag_factor, identity, left_side=True, lower=...  20 us
    concatenate x1, other arithmetic, leading_factor(): return (jnp.concatenate(lower_rows, 0), jnp.concatenate(inverse_rows, 0))  19.9 us
  transfers between devices with their start and end apart: 1, of which 1 were waited for; matrix products, arithmetic and copies ran while one was open for 7% of the time, Pallas kernels for 0%

profile of v1, /device:TPU:1, one launch (start us, length us, event | category | flops | bytes accessed | tf_op | source)
XLA Modules:
  0.0 862.7 jit_solution(14922558494883323160)
XLA Ops:
  2.1 16.0 %all_gather.3 = s32[4096,18]{0,1:T(8,128)S(1)} all-gather(s32[512,18]{0,1:T(8,128)S(1)} %pad_add_fusion), channel_id=1, replica_groups=mesh['row'=8,'col'=32] {'row'}, dimensions={0}, use_global_device_ids=true | all-gather | bytes 331776 | tf_op jit(solution)/shard_map/all_gather | solution.py:20
  20.0 18.3 %fusion.28 = f32[1536,1536]{0,1:T(8,128)S(1)} fusion(s32[1536]{0:T(1024)S(1)} %slice.297, s32[1536]{0:T(1024)S(1)} %slice.295, f32[1536]{0:T(1024)S(1)} %select_select_fusion.5, s32[1536]{0:T(1024)S(1)} %slice.293), kind=kLoop, calls=%fused_computation.64 | loop fusion | flops 108527616 | bytes 9461760 | tf_op jit(solution)/shard_map/add | solution.py:142
  38.4 3.6 copy-done
  43.9 11.7 %cholesky.374 = f32[128,128]{1,0:T(8,128)S(1)} custom-call(f32[128,128]{1,0:T(8,128)S(1)} %cholesky.586), custom_call_target="Cholesky" | custom-call | tf_op jit(solution)/shard_map/jit(cholesky)/cholesky | solution.py:70
  55.6 9.8 %custom-call.31 = f32[1,128,128]{1,2,0:T(8,128)S(1)} custom-call(f32[1,128,128]{2,1,0:T(8,128)S(1)} %get-tuple-element.310), custom_call_target="InvertDiagBlocksLowerTriangular" | custom-call | tf_op jit(solution)/shard_map/jit(cholesky)/cholesky | solution.py:70
  66.9 11.7 %cholesky.393 = f32[128,128]{1,0:T(8,128)S(1)} custom-call(f32[128,128]{1,0:T(8,128)S(1)} %cholesky.590), custom_call_target="Cholesky" | custom-call | tf_op jit(solution)/shard_map/jit(cholesky)/cholesky | solution.py:70
  78.7 10.2 %custom-call.32 = f32[1,128,128]{1,2,0:T(8,128)S(1)} custom-call(f32[1,128,128]{2,1,0:T(8,128)S(1)} %get-tuple-element.307), custom_call_target="InvertDiagBlocksLowerTriangular" | custom-call | tf_op jit(solution)/shard_map/jit(cholesky)/cholesky | solution.py:70
  90.4 11.7 %cholesky.414 = f32[128,128]{1,0:T(8,128)S(1)} custom-call(f32[128,128]{1,0:T(8,128)S(1)} %cholesky.595), custom_call_target="Cholesky" | custom-call | tf_op jit(solution)/shard_map/jit(cholesky)/cholesky | solution.py:70
  102.9 9.8 %custom-call.33 = f32[1,128,128]{1,2,0:T(8,128)S(1)} custom-call(f32[1,128,128]{2,1,0:T(8,128)S(1)} %get-tuple-element.304), custom_call_target="InvertDiagBlocksLowerTriangular" | custom-call | tf_op jit(solution)/shard_map/jit(cholesky)/cholesky | solution.py:70
  113.3 11.7 %cholesky.431 = f32[128,128]{1,0:T(8,128)S(1)} custom-call(f32[128,128]{1,0:T(8,128)S(1)} %convolution_subtract_fusion.19), custom_call_target="Cholesky" | custom-call | tf_op jit(solution)/shard_map/jit(cholesky)/cholesky | solution.py:70
  131.1 8.0 while.22
  139.1 39.3 %custom-call.34 = f32[4,128,128]{1,2,0:T(8,128)S(1)} custom-call(f32[4,128,128]{2,1,0:T(8,128)S(1)} %get-tuple-element.206), custom_call_target="InvertDiagBlocksLowerTriangular" | custom-call | tf_op jit(solution)/shard_map/triangular_solve/custom-call.3 | solution.py:71
  181.6 5.2 fusion.82
  186.9 2.9 fusion.314
  189.8 9.2 %slice_subtract_fusion = f32[1024,1024]{0,1:T(8,128)S(1)} fusion(f32[1536,1536]{0,1:T(8,128)} %copy-done, f32[1024,512]{0,1:T(8,128)S(1)} %fusion.82), kind=kOutput, calls=%fused_computation.90 | convolution fusion | flops 6443499520 | bytes 12582912 | tf_op jit(solution)/shard_map/dot_general | solution.py:84
  202.1 2.5 copy.44
  207.4 11.7 %cholesky.446 = f32[128,128]{1,0:T(8,128)S(1)} custom-call(f32[128,128]{1,0:T(8,128)S(1)} %cholesky.599), custom_call_target="Cholesky" | custom-call | tf_op jit(solution)/shard_map/jit(cholesky)/cholesky | solution.py:70
  219.7 10.6 %custom-call.35 = f32[1,128,128]{1,2,0:T(8,128)S(1)} custom-call(f32[1,128,128]{2,1,0:T(8,128)} %get-tuple-element.300), custom_call_target="InvertDiagBlocksLowerTriangular" | custom-call | tf_op jit(solution)/shard_map/jit(cholesky)/cholesky | solution.py:70
  236.3 3.9 fusion.312
  242.2 11.9 %cholesky.465 = f32[128,128]{1,0:T(8,128)S(1)} custom-call(f32[128,128]{1,0:T(8,128)S(1)} %cholesky.603), custom_call_target="Cholesky" | custom-call | tf_op jit(solution)/shard_map/jit(cholesky)/cholesky | solution.py:70
  257.7 9.8 %custom-call.36 = f32[1,128,128]{1,2,0:T(8,128)S(1)} custom-call(f32[1,128,128]{2,1,0:T(8,128)S(1)} %get-tuple-element.297), custom_call_target="InvertDiagBlocksLowerTriangular" | custom-call | tf_op jit(solution)/shard_map/jit(cholesky)/cholesky | solution.py:70
  270.8 11.7 %cholesky.486 = f32[128,128]{1,0:T(8,128)S(1)} custom-call(f32[128,128]{1,0:T(8,128)S(1)} %cholesky.608), custom_call_target="Cholesky" | custom-call | tf_op jit(solution)/shard_map/jit(cholesky)/cholesky | solution.py:70
  283.9 9.8 %custom-call.37 = f32[1,128,128]{1,2,0:T(8,128)S(1)} custom-call(f32[1,128,128]{2,1,0:T(8,128)S(1)} %get-tuple-element.294), custom_call_target="InvertDiagBlocksLowerTriangular" | custom-call | tf_op jit(solution)/shard_map/jit(cholesky)/cholesky | solution.py:70
  296.0 12.1 %cholesky.503 = f32[128,128]{1,0:T(8,128)S(1)} custom-call(f32[128,128]{1,0:T(8,128)S(1)} %convolution_subtract_fusion.18), custom_call_target="Cholesky" | custom-call | tf_op jit(solution)/shard_map/jit(cholesky)/cholesky | solution.py:70
  311.9 2.8 fusion.114
  314.7 12.0 %while.23 = (s32[]{:T(128)}, f32[512,512]{1,0:T(8,128)}, s32[4,2]{0,1:T(2,128)S(1)}, f32[4,128,128]{2,1,0:T(8,128)S(1)}, s32[]{:T(128)}) while((s32[]{:T(128)}, f32[512,512]{1,0:T(8,128)}, s32[4,2]{0,1:T(2,128)S(1)}, f32[4,128,128]{2,1,0:T(8,128)S(1)}, s32[]{:T(128)}) %tuple.135), condition=%wide.while_cond.2.clone, body=%wide.while_body.2.clone.sunk | while | flops 2 | bytes 131181 | solution.py:71
  315.4 2.3 bitcast_dynamic-update-slice_fusion.7
  318.4 2.3 bitcast_dynamic-update-slice_fusion.7
  321.4 2.3 bitcast_dynamic-update-slice_fusion.7
  324.4 2.2 bitcast_dynamic-update-slice_fusion.7
  326.7 39.9 %custom-call.38 = f32[4,128,128]{1,2,0:T(8,128)} custom-call(f32[4,128,128]{2,1,0:T(8,128)S(1)} %get-tuple-element.207), custom_call_target="InvertDiagBlocksLowerTriangular" | custom-call | tf_op jit(solution)/shard_map/triangular_solve/custom-call.3 | solution.py:71
  376.0 3.2 fusion.108
  379.3 4.1 convolution_subtract_fusion.1
  383.4 2.5 copy.50
  388.7 11.7 %cholesky.518 = f32[128,128]{1,0:T(8,128)S(1)} custom-call(f32[128,128]{1,0:T(8,128)S(1)} %cholesky.612), custom_call_target="Cholesky" | custom-call | tf_op jit(solution)/shard_map/jit(cholesky)/cholesky | solution.py:70
  401.1 10.8 %custom-call.39 = f32[1,128,128]{1,2,0:T(8,128)S(1)} custom-call(f32[1,128,128]{2,1,0:T(8,128)} %get-tuple-element.290), custom_call_target="InvertDiagBlocksLowerTriangular" | custom-call | tf_op jit(solution)/shard_map/jit(cholesky)/cholesky | solution.py:70
  417.9 4.0 fusion.223
  426.9 4.4 convolution_negate_fusion.2
  431.4 11.7 %cholesky.537 = f32[128,128]{1,0:T(8,128)S(1)} custom-call(f32[128,128]{1,0:T(8,128)S(1)} %slice-done), custom_call_target="Cholesky" | custom-call | tf_op jit(solution)/shard_map/jit(cholesky)/cholesky | solution.py:70
  445.3 10.0 %custom-call.40 = f32[1,128,128]{1,2,0:T(8,128)S(1)} custom-call(f32[1,128,128]{2,1,0:T(8,128)S(1)} %get-tuple-element.287), custom_call_target="InvertDiagBlocksLowerTriangular" | custom-call | tf_op jit(solution)/shard_map/jit(cholesky)/cholesky | solution.py:70
  458.4 13.2 %cholesky.558 = f32[128,128]{1,0:T(8,128)} custom-call(f32[128,128]{1,0:T(8,128)} %cholesky.621), custom_call_target="Cholesky" | custom-call | tf_op jit(solution)/shard_map/jit(cholesky)/cholesky | solution.py:70
  473.8 11.3 %custom-call.41 = f32[1,128,128]{1,2,0:T(8,128)} custom-call(f32[1,128,128]{2,1,0:T(8,128)} %get-tuple-element.284), custom_call_target="InvertDiagBlocksLowerTriangular" | custom-call | tf_op jit(solution)/shard_map/jit(cholesky)/cholesky | solution.py:70
  487.3 11.7 %cholesky.575 = f32[128,128]{1,0:T(8,128)S(1)} custom-call(f32[128,128]{1,0:T(8,128)S(1)} %convolution_subtract_fusion.17), custom_call_target="Cholesky" | custom-call | tf_op jit(solution)/shard_map/jit(cholesky)/cholesky | solution.py:70
  503.8 11.3 %while.24 = (s32[]{:T(128)}, f32[512,512]{1,0:T(8,128)}, s32[4,2]{0,1:T(2,128)S(1)}, f32[4,128,128]{2,1,0:T(8,128)S(1)}, s32[]{:T(128)}) while((s32[]{:T(128)}, f32[512,512]{1,0:T(8,128)}, s32[4,2]{0,1:T(2,128)S(1)}, f32[4,128,128]{2,1,0:T(8,128)S(1)}, s32[]{:T(128)}) %tuple.136), condition=%wide.while_cond.2.clone.1, body=%wide.while_body.2.clone.1.sunk | while | flops 2 | bytes 131181 | solution.py:71
  515.0 39.7 %custom-call.42 = f32[4,128,128]{1,2,0:T(8,128)S(1)} custom-call(f32[4,128,128]{2,1,0:T(8,128)S(1)} %get-tuple-element.208), custom_call_target="InvertDiagBlocksLowerTriangular" | custom-call | tf_op jit(solution)/shard_map/triangular_solve/custom-call.3 | solution.py:71
  562.5 3.5 convolution_add_fusion
  567.9 2.9 convolution_negate_fusion
  571.9 2.5 copy.68
  574.4 2.5 copy.69
  577.1 19.9 %fusion.38 = f32[1536,1536]{1,0:T(8,128)} fusion(f32[512,512]{1,0:T(8,128)S(1)} %cholesky.441, f32[512,512]{1,0:T(8,128)} %pad_maximum_fusion.1, f32[128,512]{1,0:T(8,128)} %copy-done.14, f32[128,512]{1,0:T(8,128)} %copy-done.12, f32[128,512]{1,0:T(8,128)S(1)} %fusion.243, f32[128,512]{1,0:T(8,128)S(1)} %fusion.205, f32[512,512]{1,0:T(8,128)} %convolution_negate_fusion, ...), kind=kLoop, calls=%fused_computation.76 | loop fusion | flops 33030144 | bytes 16777216 | tf_op jit(solution)/shard_map/concatenate | solution.py:122
  597.0 13.2 %fusion.140 = f32[96,1536]{1,0:T(8,128)S(1)} fusion(f32[1536,1536]{1,0:T(8,128)} %fusion.38, s32[1536]{0:T(1024)S(1)} %copy-done.30, s32[96]{0:T(128)S(1)} %sub.151, s32[1536]{0:T(1024)S(1)} %copy-done.28, s32[96]{0:T(128)S(1)} %sub.147, f32[1536]{0:T(1024)S(1)} %select_select_fusion.5, f32[96]{0:T(128)S(1)} %compare_select_fusion.1, ...), kind=kOutput, calls=%fused_computation.241 | convolution fusion | flops 2724249600 | bytes 10053120 | tf_op jit(solution)/shard_map/dot_general | solution.py:155
  614.8 4.8 stack.2
  619.7 10.2 %all-to-all-start = ((bf16[32,6,16,1536]{3,2,1,0:T(8,128)(2,1)}), bf16[32,6,16,1536]{3,2,1,0:T(8,128)(2,1)}, u32[]{:S(2)}, u32[]{:S(2)}) async-start(bf16[32,6,16,1536]{3,2,1,0:T(8,128)(2,1)} %stack.2), calls=%async_computation | async-start | bytes 18874368 | tf_op jit(solution)/shard_map/all_to_all | solution.py:188
  632.1 28.1 %fusion.79 = bf16[512,1536,1]{1,0,2:T(8,128)(2,1)S(1)} fusion(f32[1536,1536]{1,0:T(8,128)} %fusion.38, s32[1536]{0:T(1024)S(1)} %copy-done.30, s32[512]{0:T(512)S(1)} %dynamic_slice.42, s32[1536]{0:T(1024)S(1)} %copy-done.28, s32[512]{0:T(512)S(1)} %dynamic_slice.41, f32[1536]{0:T(1024)S(1)} %select_select_fusion.5, f32[512]{0:T(512)S(1)} %get-tuple-element.255, ...), kind=kOutput, calls=%fused_computation.131 | convolution fusion | flops 14530117632 | bytes 11042816 | tf_op jit(solution)/shard_map/dot_general | solution.py:184
  660.2 40.1 %while.21 = (s32[]{:T(128)}, f32[6,512,512]{2,1,0:T(8,128)}, s32[6]{0:T(128)S(1)}, s32[]{:T(128)}, s32[]{:T(128)}, /*index=5*/s32[6,512]{1,0:T(8,128)}, s32[512]...) while((s32[]{:T(128)}, f32[6,512,512]{2,1,0:T(8,128)}, ...), condition=%wide.region_9.12_spmd.clone, body=%wide.region_8.11_spmd.clone.sunk | while | flops 12324872 | bytes 1135325 | solution.py:182
  664.1 3.0 fusion.358
  670.8 3.0 fusion.358
  677.4 3.0 fusion.358
  684.1 3.0 fusion.358
  690.7 3.0 fusion.358
  697.4 3.0 fusion.358
  700.4 141.9 %all-to-all-done = bf16[32,6,16,1536]{3,2,1,0:T(8,128)(2,1)} async-done(((bf16[32,6,16,1536]{3,2,1,0:T(8,128)(2,1)}), bf16[32,6,16,1536]{3,2,1,0:T(8,128)(2,1)}, u32[]{:S(2)}, u32[]{:S(2)}) %all-to-all-start) | async-done | bytes 9437216 | tf_op jit(solution)/shard_map/all_to_all | solution.py:188
  842.2 8.5 copy.58
  850.8 11.6 %convolution_subtract_fusion = f32[6,512,512]{2,1,0:T(8,128)} fusion(f32[6,512,512]{2,1,0:T(8,128)} %get-tuple-element.163, bf16[6,512,1536]{2,1,0:T(8,128)(2,1)} %bitcast.182, bf16[512,1536,1]{1,0,2:T(8,128)(2,1)S(1)} %fusion.79), kind=kOutput, calls=%fused_computation.132 | convolution fusion | flops 4833411072 | bytes 23592960 | tf_op jit(solution)/shard_map/sik,jk->sij/dot_general | solution.py:185
  (253 shorter events, 125.5 us)
Async XLA Ops:
  18.2 0.6 copy-start.24
  18.3 25.6 %copy-start.25 = (s32[1536]{0:T(1024)}, s32[1536]{0:T(1024)S(1)}, u32[]{:S(2)}) copy-start(s32[1536]{0:T(1024)S(1)} %slice.293) | copy-start | bytes 18436
  19.0 354.1 %copy-start.2 = (f32[512,512]{1,0:T(8,128)}, f32[512,512]{1,0:T(8,128)S(1)}, u32[]{:S(2)}) copy-start(f32[512,512]{1,0:T(8,128)S(1)} %fusion.116) | copy-start | bytes 3145732
  19.1 0.8 copy-start.31
  19.1 46.8 %copy-start.27 = (s32[1536]{0:T(1024)}, s32[1536]{0:T(1024)S(1)}, u32[]{:S(2)}) copy-start(s32[1536]{0:T(1024)S(1)} %slice.295) | copy-start | bytes 18436
  20.0 18.4 %copy-start.32 = (s32[24576]{0:T(1024)}, s32[24576]{0:T(1024)S(1)}, u32[]{:S(2)}) copy-start(s32[24576]{0:T(1024)S(1)} %reshape_squeeze.7) | copy-start | bytes 294916
  20.0 45.9 %copy-start.29 = (s32[1536]{0:T(1024)}, s32[1536]{0:T(1024)S(1)}, u32[]{:S(2)}) copy-start(s32[1536]{0:T(1024)S(1)} %slice.297) | copy-start | bytes 18436
  38.4 3.6 copy-start
  66.3 0.7 copy-start.22
  178.8 57.5 %copy-start.4 = (f32[128,512]{1,0:T(8,128)}, f32[128,512]{1,0:T(8,128)S(1)}, u32[]{:S(2)}) copy-start(f32[128,512]{1,0:T(8,128)S(1)} %fusion.209) | copy-start | bytes 786436
  179.7 7.2 copy-start.7
  180.5 6.3 copy-start.10
  181.6 5.3 copy-start.13
  199.0 2.0 copy-start.1
  206.4 1.0 copy-start.19
  370.4 5.7 copy-start.5
  373.1 6.2 copy-start.8
  376.0 3.2 copy-start.11
  387.7 1.0 copy-start.18
  417.9 13.6 %slice-start = ((f32[384,128]{1,0:T(8,128)}), f32[128,128]{1,0:T(8,128)S(1)}, s32[]{:S(2)}) async-start(f32[384,128]{1,0:T(8,128)} %convolution_subtract_fusion.11), calls=%async_computation.1 | async-start | bytes 131072 | tf_op jit(solution)/shard_map/jit(cholesky)/cholesky | solution.py:70
  426.9 127.8 %copy-start.3 = (f32[512,512]{1,0:T(8,128)S(1)}, f32[512,512]{1,0:T(8,128)}, u32[]{:S(2)}) copy-start(f32[512,512]{1,0:T(8,128)} %copy-done.2) | copy-start | bytes 3145732
  503.7 67.8 %copy-start.21 = (s32[2,6,512]{2,0,1:T(2,128)S(1)}, s32[2,6,512]{2,0,1:T(2,128)}, u32[]{:S(2)}) copy-start(s32[2,6,512]{2,0,1:T(2,128)} %param.11) | copy-start | bytes 73732
  554.8 2.1 copy-start.23
  554.8 13.1 %copy-start.15 = (f32[512,512]{1,0:T(8,128)S(1)}, f32[512,512]{1,0:T(8,128)}, u32[]{:S(2)}) copy-start(f32[512,512]{1,0:T(8,128)} %fusion.223) | copy-start | bytes 3145732
  558.2 18.9 %copy-start.6 = (f32[128,512]{1,0:T(8,128)S(1)}, f32[128,512]{1,0:T(8,128)}, u32[]{:S(2)}) copy-start(f32[128,512]{1,0:T(8,128)} %copy-done.5) | copy-start | bytes 786436
  558.2 18.9 %copy-start.9 = (f32[128,512]{1,0:T(8,128)S(1)}, f32[128,512]{1,0:T(8,128)}, u32[]{:S(2)}) copy-start(f32[128,512]{1,0:T(8,128)} %copy-done.8) | copy-start | bytes 786436
  559.6 8.3 copy-start.12
  562.5 14.5 %copy-start.14 = (f32[128,512]{1,0:T(8,128)}, f32[128,512]{1,0:T(8,128)S(1)}, u32[]{:S(2)}) copy-start(f32[128,512]{1,0:T(8,128)S(1)} %fusion.240) | copy-start | bytes 786436
  577.0 20.0 %copy-start.26 = (s32[1536]{0:T(1024)S(1)}, s32[1536]{0:T(1024)}, u32[]{:S(2)}) copy-start(s32[1536]{0:T(1024)} %copy-done.25) | copy-start | bytes 18436
  577.0 20.0 %copy-start.28 = (s32[1536]{0:T(1024)S(1)}, s32[1536]{0:T(1024)}, u32[]{:S(2)}) copy-start(s32[1536]{0:T(1024)} %copy-done.27) | copy-start | bytes 18436
  577.0 20.0 %copy-start.30 = (s32[1536]{0:T(1024)S(1)}, s32[1536]{0:T(1024)}, u32[]{:S(2)}) copy-start(s32[1536]{0:T(1024)} %copy-done.29) | copy-start | bytes 18436
  597.0 14.9 %copy-start.16 = (f32[512,512]{1,0:T(8,128)S(1)}, f32[512,512]{1,0:T(8,128)}, u32[]{:S(2)}) copy-start(f32[512,512]{1,0:T(8,128)} %get-tuple-element.264) | copy-start | bytes 3145732
  597.0 14.9 %copy-start.17 = (f32[512,512]{1,0:T(8,128)S(1)}, f32[512,512]{1,0:T(8,128)}, u32[]{:S(2)}) copy-start(f32[512,512]{1,0:T(8,128)} %get-tuple-element.262) | copy-start | bytes 3145732
  610.3 0.8 copy-start.20
  619.7 222.6 %all-to-all-start = ((bf16[32,6,16,1536]{3,2,1,0:T(8,128)(2,1)}), bf16[32,6,16,1536]{3,2,1,0:T(8,128)(2,1)}, u32[]{:S(2)}, u32[]{:S(2)}) async-start(bf16[32,6,16,1536]{3,2,1,0:T(8,128)(2,1)} %stack.2), calls=%async_computation | async-start | bytes 18874368 | tf_op jit(solution)/shard_map/all_to_all | solution.py:188
